TPU v7x, 32 devices: a whole 2x2x4 slice. The times are simulated.
32 devices in a mesh: gx: 8 (over z, y), gy: 4 (over x, core).
Axes of the slice: x: 2, y: 2, z: 4, core: 2. Of those that a mesh axis runs over, the one named last changes fastest.
Arguments:
- vorticity_grid: float32 [4096, 4096], P(('gx', 'gy')), may hold values from -6 to 6
- forcing_grid: float32 [4096, 4096], P(('gx', 'gy')), may hold values from -12 to 12
- cutoff: int32 [1], replicated, may hold values from 853 to 1365
- forcing_shells: int32 [4], replicated, may hold values from 2 to 127
Outputs:
- lifted_spectrum: float32 [2, 4096, 4096], P(None, ('gx', 'gy'))
- coarse_field: float32 [256, 256], P(('gx', 'gy'))
Inputs may be any that keep to these rules, and one draw needn't show every extreme that they name: Nonlinear modes with an absolute wavenumber index above cutoff are removed.
All inputs are finite; a program needn't handle non-finite values.
Results may differ from a plain program's by a relative error of at most 0.0001.
Values sent between devices are 32-bit elements; how exact they have to be, the bound alone decides.
A program may use at most 128 MiB of HBM per device.

v0:
```python
import math
import jax
import jax.numpy as jnp
from jax import lax
from jax.sharding import PartitionSpec as P

RADIX = 64
LOW = 256
SHELLS = 4
time_step = 0.05
viscosity = 0.05
coarse_ratio = 4.0


def signed_index(index_array, length_of):
    return jnp.where(index_array < length_of // 2, index_array, index_array - length_of)


def pair_tables(first_ids, second_ids, length_of):
    product = first_ids[:, None] * second_ids[None, :] % length_of
    phases = 2.0 * math.pi / length_of * product.astype(jnp.float32)
    factor = 1.0 / math.sqrt(length_of)
    return (jnp.cos(phases) * factor, jnp.sin(phases) * factor)


def contract(pattern, left_side, right_side):
    return jnp.einsum(pattern, left_side, right_side, precision=lax.Precision.HIGHEST)


def complex_table(direction):
    indices = jnp.arange(RADIX, dtype=jnp.int32)
    cos_table, sin_table = pair_tables(indices, indices, RADIX)
    signed_sin = direction * sin_table
    from_real = jnp.stack([cos_table, signed_sin], axis=1)
    from_imag = jnp.stack([-signed_sin, cos_table], axis=1)
    return jnp.stack([from_real, from_imag], axis=0)


def dft_last(values, direction, is_real):
    length_of = values.shape[-1]
    table = complex_table(direction)
    if is_real:
        leading = values.shape[:-1]
        split_values = values.reshape(leading + (RADIX, RADIX))
        first = contract("...ab,adk->d...kb", split_values, table[0])
    else:
        leading = values.shape[1:-1]
        split_values = values.reshape((2,) + leading + (RADIX, RADIX))
        first = contract("c...ab,cadk->d...kb", split_values, table)
    indices = jnp.arange(RADIX, dtype=jnp.int32)
    twiddle_index = indices[:, None] * indices[None, :] % length_of
    twiddle_phase = 2.0 * math.pi / length_of * twiddle_index.astype(jnp.float32)
    twiddle_real = jnp.cos(twiddle_phase)
    twiddle_imag = direction * jnp.sin(twiddle_phase)
    turned = jnp.stack(
        [
            first[0] * twiddle_real - first[1] * twiddle_imag,
            first[0] * twiddle_imag + first[1] * twiddle_real,
        ]
    )
    final = contract("c...kb,cbdj->d...jk", turned, table)
    return final.reshape((2,) + leading + (length_of,))


def rows_to_grid(packed):
    return lax.all_to_all(packed, ("gx", "gy"), split_axis=1, concat_axis=2, tiled=True)


def rows_to_waves(packed):
    return lax.all_to_all(packed, ("gx", "gy"), split_axis=2, concat_axis=1, tiled=True)


def forward(fields):
    field_count = fields.shape[0]
    half = dft_last(fields, -1.0, True)
    moved = rows_to_waves(half.reshape((2 * field_count,) + half.shape[2:]))
    moved = jnp.swapaxes(moved, 1, 2)
    return dft_last(moved.reshape((2, field_count) + moved.shape[1:]), -1.0, False)


def inverse(spectra):
    field_count = spectra.shape[1]
    half = dft_last(spectra, 1.0, False)
    packed = jnp.swapaxes(half.reshape((2 * field_count,) + half.shape[2:]), 1, 2)
    moved = rows_to_grid(packed)
    return dft_last(moved.reshape((2, field_count) + moved.shape[1:]), 1.0, False)


def body(vorticity_grid, forcing_grid, cutoff, forcing_shells):
    row_count = vorticity_grid.shape[0]
    grid_size = vorticity_grid.shape[1]
    device_rank = lax.axis_index("gx") * lax.axis_size("gy") + lax.axis_index("gy")
    device_total = lax.axis_size("gx") * lax.axis_size("gy")
    row_start = device_rank * row_count
    row_ids = row_start + jnp.arange(row_count, dtype=jnp.int32)
    col_ids = jnp.arange(grid_size, dtype=jnp.int32)
    wave_y = signed_index(row_ids, grid_size)[:, None]
    wave_x = signed_index(col_ids, grid_size)[None, :]
    wave_unit = 2.0 * math.pi / grid_size
    deriv_y = (
        jnp.where(row_ids[:, None] == grid_size // 2, 0, wave_y).astype(jnp.float32) * wave_unit
    )
    deriv_x = (
        jnp.where(col_ids[None, :] == grid_size // 2, 0, wave_x).astype(jnp.float32) * wave_unit
    )
    squares = wave_x * wave_x + wave_y * wave_y
    laplace = squares.astype(jnp.float32) * (wave_unit * wave_unit)
    inverse_lap = jnp.where(squares == 0, 0.0, 1.0 / jnp.maximum(laplace, wave_unit * wave_unit))
    dealias = (jnp.abs(wave_x) <= cutoff[0]) & (jnp.abs(wave_y) <= cutoff[0])
    shell_mask = jnp.zeros((row_count, grid_size), dtype=bool)
    for shell_index in range(SHELLS):
        radius = forcing_shells[shell_index]
        shell_mask = shell_mask | (radius * radius <= squares) & (
            squares < (radius + 1) * (radius + 1)
        )
    started = forward(jnp.stack([vorticity_grid, forcing_grid]))
    drive_real = jnp.where(shell_mask, started[0, 1], 0.0)
    drive_imag = jnp.where(shell_mask, started[1, 1], 0.0)
    state_real = started[0, 0]
    state_imag = started[1, 0]

    def tendency(now_real, now_imag):
        stream_real = now_real * inverse_lap
        stream_imag = now_imag * inverse_lap
        speed_real = deriv_x * stream_real - deriv_y * stream_imag
        speed_imag = deriv_x * stream_imag + deriv_y * stream_real
        slope_real = -deriv_y * now_real - deriv_x * now_imag
        slope_imag = -deriv_y * now_imag + deriv_x * now_real
        spectra = jnp.stack(
            [jnp.stack([speed_real, slope_real]), jnp.stack([speed_imag, slope_imag])]
        )
        grids = inverse(spectra)
        advect = grids[0, 0] * grids[0, 1] + grids[1, 0] * grids[1, 1]
        term = forward(advect[None])
        out_real = (
            -jnp.where(dealias, term[0, 0], 0.0) - viscosity * laplace * now_real + drive_real
        )
        out_imag = (
            -jnp.where(dealias, term[1, 0], 0.0) - viscosity * laplace * now_imag + drive_imag
        )
        return (out_real, out_imag)

    earlier_real = state_real
    earlier_imag = state_imag
    first_real, first_imag = tendency(state_real, state_imag)
    second_real, second_imag = tendency(
        state_real + time_step * first_real, state_imag + time_step * first_imag
    )
    state_real = state_real + 0.5 * time_step * (first_real + second_real)
    state_imag = state_imag + 0.5 * time_step * (first_imag + second_imag)
    projected_real = state_real + coarse_ratio * (state_real - earlier_real)
    projected_imag = state_imag + coarse_ratio * (state_imag - earlier_imag)
    half_low = LOW // 2
    low_modes = (
        (wave_x >= -half_low) & (wave_x < half_low) & (wave_y >= -half_low) & (wave_y < half_low)
    )
    lifted_real = jnp.where(low_modes, projected_real, state_real)
    lifted_imag = jnp.where(low_modes, projected_imag, state_imag)
    projected = jnp.stack([projected_real, projected_imag])
    low_columns = jnp.concatenate(
        [projected[:, :, :half_low], projected[:, :, grid_size - half_low :]], axis=2
    )
    block_ids = jnp.arange(LOW, dtype=jnp.int32)
    coarse_rows = LOW // device_total
    every_row = lax.all_gather(low_columns, ("gx", "gy"), axis=1, tiled=True)
    block_low = jnp.concatenate(
        [every_row[:, :half_low], every_row[:, grid_size - half_low :]], axis=1
    )
    own_ids = device_rank * coarse_rows + jnp.arange(coarse_rows, dtype=jnp.int32)
    column_cos, column_sin = pair_tables(block_ids, own_ids, LOW)
    mixed_real = contract("qp,pa->qa", block_low[0], column_cos) - contract(
        "qp,pa->qa", block_low[1], column_sin
    )
    mixed_imag = contract("qp,pa->qa", block_low[0], column_sin) + contract(
        "qp,pa->qa", block_low[1], column_cos
    )
    row_cos, row_sin = pair_tables(block_ids, block_ids, LOW)
    coarse = contract("qa,qb->ab", mixed_real, row_cos) - contract("qa,qb->ab", mixed_imag, row_sin)
    return (jnp.stack([lifted_real, lifted_imag]), coarse)


def solution(mesh):
    placed = (P(("gx", "gy"), None), P(("gx", "gy"), None), P(), P())
    return jax.shard_map(
        body,
        mesh=mesh,
        in_specs=placed,
        out_specs=(P(None, ("gx", "gy"), None), P(("gx", "gy"), None)),
        check_vma=False,
    )
```

profile of v0, /device:TPU:0, one launch (start us, length us, event | category | flops | bytes accessed | tf_op | source)
XLA Modules:
  0.0 1329.7 jit_solution(10226126901157418966)
XLA Ops:
  26.6 12.5 fusion.62
  44.0 18.6 %copy.179 = f32[4,128,4096]{1,0,2:T(4,128)} copy(f32[4,128,4096]{1,2,0:T(8,128)S(1)} %bitcast.399) | data formatting | bytes 16777216 | tf_op jit(solution)/shard_map/reshape;reshape | solution.py:76
  70.7 185.6 %all-to-all-done = f32[4,128,4096]{1,0,2:T(4,128)} async-done(((f32[4,128,4096]{1,0,2:T(4,128)}), f32[4,128,4096]{1,0,2:T(4,128)}, u32[]{:S(2)}, u32[]{:S(2)}) %all-to-all-start) | async-done | bytes 8388640 | tf_op jit(solution)/shard_map/all_to_all | solution.py:70
  263.5 9.0 copy.181
  272.4 15.8 %fusion.65 = f32[2,2,128,64,64]{2,3,4,1,0:T(8,128)S(1)} fusion(f32[2,2,128,64,64]{2,4,3,1,0:T(8,128)} %bitcast.401, f32[2,64,2,64,1,1]{1,3,2,0,5,4:T(8,128)S(1)} %get-tuple-element.58), kind=kOutput, calls=%fused_computation.112 | convolution fusion | flops 3221225472 | bytes 16842752 | tf_op jit(solution)/shard_map/c...ab,cadk->d...kb/dot_general | solution.py:27
  291.7 12.5 fusion.68
  330.7 12.7 fusion.71
  348.3 17.8 %copy.197 = f32[4,4096,128]{2,0,1:T(4,128)S(1)} copy(f32[4,4096,128]{2,1,0:T(8,128)S(1)} %bitcast.402) | data formatting | bytes 16777216 | tf_op jit(solution)/shard_map/transpose | solution.py:84
  366.1 185.3 %all_to_all.84 = f32[4,4096,128]{2,0,1:T(4,128)S(1)} all-to-all(f32[4,4096,128]{2,0,1:T(4,128)S(1)} %copy.197), channel_id=1, replica_groups=mesh['gx'=8,'gy'=4] {'gx','gy'}, dimensions={1} | all-to-all | bytes 16777216 | tf_op jit(solution)/shard_map/all_to_all | solution.py:66
  555.2 9.0 copy.199
  564.1 15.8 %fusion.74 = f32[2,2,128,64,64]{2,3,4,1,0:T(8,128)S(1)} fusion(f32[2,2,128,64,64]{2,4,3,1,0:T(8,128)} %bitcast.404, f32[1,64,2,64]{1,3,2,0:T(8,128)S(1)} %get-tuple-element.60, f32[1,64,2,64]{1,3,2,0:T(8,128)S(1)} %get-tuple-element.59), kind=kOutput, calls=%fused_computation.115 | convolution fusion | flops 3221241856 | bytes 16842752 | tf_op jit(solution)/shard_map/c...ab,cadk->d...kb/dot_general | solution.py:27
  583.4 12.5 fusion.77
  616.5 16.1 %copy.209 = f32[2,128,4096]{1,0,2:T(2,128)} copy(f32[2,128,4096]{1,2,0:T(8,128)S(1)} %bitcast.412) | data formatting | bytes 8388608 | tf_op jit(solution)/shard_map/reshape;reshape | solution.py:76
  645.7 84.6 %all-to-all-done.2 = f32[2,128,4096]{1,0,2:T(2,128)} async-done(((f32[2,128,4096]{1,0,2:T(2,128)}), f32[2,128,4096]{1,0,2:T(2,128)}, u32[]{:S(2)}, u32[]{:S(2)}) %all-to-all-start.2) | async-done | bytes 4194336 | tf_op jit(solution)/shard_map/all_to_all | solution.py:70
  757.3 10.4 multiply_subtract_fusion.9
  781.6 12.5 fusion.80
  799.0 17.8 %copy.228 = f32[4,4096,128]{2,0,1:T(4,128)S(1)} copy(f32[4,4096,128]{2,1,0:T(8,128)S(1)} %bitcast.405) | data formatting | bytes 16777216 | tf_op jit(solution)/shard_map/transpose | solution.py:84
  816.8 187.4 %all_to_all.85 = f32[4,4096,128]{2,0,1:T(4,128)S(1)} all-to-all(f32[4,4096,128]{2,0,1:T(4,128)S(1)} %copy.228), channel_id=1, replica_groups=mesh['gx'=8,'gy'=4] {'gx','gy'}, dimensions={1} | all-to-all | bytes 16777216 | tf_op jit(solution)/shard_map/all_to_all | solution.py:66
  1008.0 9.0 copy.230
  1017.0 15.8 %fusion.83 = f32[2,2,128,64,64]{2,3,4,1,0:T(8,128)S(1)} fusion(f32[2,2,128,64,64]{2,4,3,1,0:T(8,128)} %bitcast.407, f32[1,64,2,64]{1,3,2,0:T(8,128)S(1)} %get-tuple-element.60, f32[1,64,2,64]{1,3,2,0:T(8,128)S(1)} %get-tuple-element.59), kind=kOutput, calls=%fused_computation.118 | convolution fusion | flops 3221241856 | bytes 16842752 | tf_op jit(solution)/shard_map/c...ab,cadk->d...kb/dot_general | solution.py:27
  1036.5 12.5 fusion.86
  1069.4 16.5 %copy.240 = f32[2,128,4096]{1,0,2:T(2,128)} copy(f32[2,128,4096]{1,2,0:T(8,128)S(1)} %bitcast.415) | data formatting | bytes 8388608 | tf_op jit(solution)/shard_map/reshape;reshape | solution.py:76
  1096.2 87.3 %all-to-all-done.4 = f32[2,128,4096]{1,0,2:T(2,128)} async-done(((f32[2,128,4096]{1,0,2:T(2,128)}), f32[2,128,4096]{1,0,2:T(2,128)}, u32[]{:S(2)}, u32[]{:S(2)}) %all-to-all-start.4) | async-done | bytes 4194336 | tf_op jit(solution)/shard_map/all_to_all | solution.py:70
  1239.2 75.9 %all-gather.2.cloned.1.call-done = f32[2,4096,256]{1,2,0:T(8,128)} async-done(((f32[2,128,256]{1,2,0:T(8,128)}), f32[2,4096,256]{1,2,0:T(8,128)}) %all-gather.2.cloned.1.call-update) | async-done | bytes 8388624 | tf_op jit(solution)/shard_map/all_gather | solution.py:165
  (125 shorter events, 253.4 us)
Async XLA Ops:
  14.1 1.6 copy-start.5
  62.6 193.7 %all-to-all-start = ((f32[4,128,4096]{1,0,2:T(4,128)}), f32[4,128,4096]{1,0,2:T(4,128)}, u32[]{:S(2)}, u32[]{:S(2)}) async-start(f32[4,128,4096]{1,0,2:T(4,128)} %copy.179), calls=%async_computation | async-start | bytes 16777216 | tf_op jit(solution)/shard_map/all_to_all | solution.py:70
  309.1 4.5 copy-start
  313.6 5.1 copy-start.2
  632.7 4.0 copy-start.10
  632.7 97.7 %all-to-all-start.2 = ((f32[2,128,4096]{1,0,2:T(2,128)}), f32[2,128,4096]{1,0,2:T(2,128)}, u32[]{:S(2)}, u32[]{:S(2)}) async-start(f32[2,128,4096]{1,0,2:T(2,128)} %copy.209), calls=%async_computation.2 | async-start | bytes 8388608 | tf_op jit(solution)/shard_map/all_to_all | solution.py:70
  750.3 0.9 copy-start.9
  751.2 6.1 copy-start.3
  751.2 6.1 copy-start.6
  751.2 6.1 copy-start.7
  757.3 10.4 copy-start.1
  1085.9 97.6 %all-to-all-start.4 = ((f32[2,128,4096]{1,0,2:T(2,128)}), f32[2,128,4096]{1,0,2:T(2,128)}, u32[]{:S(2)}, u32[]{:S(2)}) async-start(f32[2,128,4096]{1,0,2:T(2,128)} %copy.240), calls=%async_computation.4 | async-start | bytes 8388608 | tf_op jit(solution)/shard_map/all_to_all | solution.py:70
  1089.8 225.3 %all-gather.2.cloned.1.call-start = ((), (), s32[]{:S(2)}) async-start(), calls=%async_computation.5 | async-start | bytes 8650752 | tf_op jit(solution)/shard_map/all_gather | solution.py:165
  1210.1 3.1 slice-start
  1210.7 3.0 slice-start.1
  1211.9 2.4 copy-start.4
  1225.0 1.7 copy-start.8
Sparse Core Ops, SparseCore 0:
  1225.9 89.2 all-gather.1
where the time goes:
time: 1340 us; the launch traced here: 1330 us
  waiting for transfers between devices  434 us (32%)
  blocking collectives  373 us (28%)
  local copies, waits for them, and re-layouts  214 us (16%)
  matrix products  202 us (15%)
  other arithmetic  67.4 us (5%)
  between operations  23.3 us (2%)
  starting transfers between devices  15.8 us (1%)
    all_to_all x2, blocking collectives, rows_to_grid(): lax.all_to_all(packed, ('gx', 'gy'), split_axis=1, concat_axis=2, tiled=T...  373 us
    all_to_all x3, waiting for transfers between devices, rows_to_waves(): lax.all_to_all(packed, ('gx', 'gy'), split_axis=2, concat_axis=1, tiled=T...  358 us
    dot_general x26, matrix products, contract(): jnp.einsum(pattern, left_side, right_side, precision=lax.Precision.HIGHEST)  202 us
    all_gather x1, waiting for transfers between devices, body(): every_row = lax.all_gather(low_columns, ('gx', 'gy'), axis=1, tiled=True)  75.9 us
    another operation x3, local copies, waits for them, and re-layouts, forward(): moved = rows_to_waves(half.reshape((2 * field_count,) + half.shape[2:]))  51.3 us
    all_to_all x6, local copies, waits for them, and re-layouts, rows_to_waves(): lax.all_to_all(packed, ('gx', 'gy'), split_axis=2, concat_axis=1, tiled=T...  36.4 us
    transpose x2, local copies, waits for them, and re-layouts, inverse(): jnp.swapaxes(half.reshape((2 * field_count,) + half.shape[2:]), 1, 2)  35.6 us
    transpose x8, local copies, waits for them, and re-layouts, contract(): jnp.einsum(pattern, left_side, right_side, precision=lax.Precision.HIGHEST)  34 us
  transfers between devices with their start and end apart: 4, of which 4 were waited for; matrix products, arithmetic and copies ran while one was open for 1% of the time, Pallas kernels for 0%

commit v1 on v0

--- a/solution.py
+++ b/solution.py
@@ -10,6 +10,12 @@
 time_step = 0.05
 viscosity = 0.05
 coarse_ratio = 4.0
+
+
+def swap_blocks(x, name, split, join):
+    parts = jnp.split(x, lax.axis_size(name), axis=split)
+    arrived = lax.all_to_all(jnp.stack(parts), name, 0, 0)
+    return jnp.concatenate(arrived, axis=join)
 
 
 def signed_index(index_array, length_of):
@@ -63,7 +69,7 @@
 
 
 def rows_to_grid(packed):
-    return lax.all_to_all(packed, ("gx", "gy"), split_axis=1, concat_axis=2, tiled=True)
+    return swap_blocks(packed, ("gx", "gy"), 1, 2)
 
 
 def rows_to_waves(packed):

time: 1340 us -> 1300 us (0.970)
  local copies, waits for them, and re-layouts: 214 us -> 173 us
    transpose x2 -> x0, local copies, waits for them, and re-layouts: 35.6 us -> none  [inverse(): jnp.swapaxes(half.reshape((2 * field_count,) + half.shape[2:]), 1, 2)]
    all_to_all x4 -> x0, local copies, waits for them, and re-layouts: 25.5 us -> none  [rows_to_grid(): lax.all_to_all(packed, ('gx', 'gy'), split_axis=1, concat_axis=2, tiled=T...]
    reshape x0 -> x2, local copies, waits for them, and re-layouts: none -> 17.9 us  [swap_blocks(): return jnp.concatenate(arrived, axis=join)]
  transfers between devices with their start and end apart: 4 -> 4, of which waited for: 4 -> 4; matrix products, arithmetic and copies ran while one was open for 1% -> 2% of each run, Pallas kernels for 0% -> 0%
where the time goes in v1:
time: 1300 us; the launch traced here: 1290 us
  waiting for transfers between devices  434 us (33%)
  blocking collectives  374 us (29%)
  matrix products  202 us (16%)
  local copies, waits for them, and re-layouts  173 us (13%)
  other arithmetic  67.4 us (5%)
  between operations  23.8 us (2%)
  starting transfers between devices  15.7 us (1%)
    all_to_all x2, blocking collectives, swap_blocks(): arrived = lax.all_to_all(jnp.stack(parts), name, 0, 0)  374 us
    all_to_all x3, waiting for transfers between devices, rows_to_waves(): lax.all_to_all(packed, ('gx', 'gy'), split_axis=2, concat_axis=1, tiled=T...  358 us
    dot_general x26, matrix products, contract(): jnp.einsum(pattern, left_side, right_side, precision=lax.Precision.HIGHEST)  202 us
    all_gather x1, waiting for transfers between devices, body(): every_row = lax.all_gather(low_columns, ('gx', 'gy'), axis=1, tiled=True)  75.9 us
    another operation x3, local copies, waits for them, and re-layouts, forward(): moved = rows_to_waves(half.reshape((2 * field_count,) + half.shape[2:]))  51.3 us
    all_to_all x6, local copies, waits for them, and re-layouts, rows_to_waves(): lax.all_to_all(packed, ('gx', 'gy'), split_axis=2, concat_axis=1, tiled=T...  36.4 us
    transpose x8, local copies, waits for them, and re-layouts, contract(): jnp.einsum(pattern, left_side, right_side, precision=lax.Precision.HIGHEST)  34 us
  transfers between devices with their start and end apart: 4, of which 4 were waited for; matrix products, arithmetic and copies ran while one was open for 2% of the time, Pallas kernels for 0%

profile of v1, /device:TPU:0, one launch (start us, length us, event | category | flops | bytes accessed | tf_op | source)
XLA Modules:
  0.0 1289.1 jit_solution(298726615774462657)
XLA Ops:
  26.6 12.5 fusion.62
  44.0 18.6 %copy.179 = f32[4,128,4096]{1,0,2:T(4,128)} copy(f32[4,128,4096]{1,2,0:T(8,128)S(1)} %bitcast.715) | data formatting | bytes 16777216 | tf_op jit(solution)/shard_map/reshape;reshape | solution.py:82
  70.7 185.6 %all-to-all-done = f32[4,128,4096]{1,0,2:T(4,128)} async-done(((f32[4,128,4096]{1,0,2:T(4,128)}), f32[4,128,4096]{1,0,2:T(4,128)}, u32[]{:S(2)}, u32[]{:S(2)}) %all-to-all-start) | async-done | bytes 8388640 | tf_op jit(solution)/shard_map/all_to_all | solution.py:76
  263.5 9.0 copy.181
  272.4 15.8 %fusion.65 = f32[2,2,128,64,64]{2,3,4,1,0:T(8,128)S(1)} fusion(f32[2,2,128,64,64]{2,4,3,1,0:T(8,128)} %bitcast.717, f32[2,64,2,64,1,1]{1,3,2,0,5,4:T(8,128)S(1)} %get-tuple-element.58), kind=kOutput, calls=%fused_computation.112 | convolution fusion | flops 3221225472 | bytes 16842752 | tf_op jit(solution)/shard_map/c...ab,cadk->d...kb/dot_general | solution.py:33
  291.7 12.5 fusion.68
  318.7 8.5 fusion.90
  330.7 12.7 fusion.71
  349.2 186.0 %all_to_all.64 = f32[32,4,128,128]{3,2,1,0:T(8,128)} all-to-all(f32[32,4,128,128]{3,2,1,0:T(8,128)S(1)} %fusion.216), channel_id=1, replica_groups=mesh['gx'=8,'gy'=4] {'gx','gy'}, dimensions={0} | all-to-all | bytes 16777216 | tf_op jit(solution)/shard_map/all_to_all | solution.py:17
  535.2 9.0 copy.197
  544.2 15.8 %fusion.74 = f32[2,2,128,64,64]{2,3,4,1,0:T(8,128)S(1)} fusion(f32[2,2,128,64,64]{2,4,3,1,0:T(8,128)} %bitcast.719, f32[1,64,2,64]{1,3,2,0:T(8,128)S(1)} %get-tuple-element.60, f32[1,64,2,64]{1,3,2,0:T(8,128)S(1)} %get-tuple-element.59), kind=kOutput, calls=%fused_computation.115 | convolution fusion | flops 3221241856 | bytes 16842752 | tf_op jit(solution)/shard_map/c...ab,cadk->d...kb/dot_general | solution.py:33
  563.4 12.5 fusion.77
  596.6 16.1 %copy.207 = f32[2,128,4096]{1,0,2:T(2,128)} copy(f32[2,128,4096]{1,2,0:T(8,128)S(1)} %bitcast.726) | data formatting | bytes 8388608 | tf_op jit(solution)/shard_map/reshape;reshape | solution.py:82
  625.7 84.6 %all-to-all-done.2 = f32[2,128,4096]{1,0,2:T(2,128)} async-done(((f32[2,128,4096]{1,0,2:T(2,128)}), f32[2,128,4096]{1,0,2:T(2,128)}, u32[]{:S(2)}, u32[]{:S(2)}) %all-to-all-start.2) | async-done | bytes 4194336 | tf_op jit(solution)/shard_map/all_to_all | solution.py:76
  737.3 10.4 multiply_subtract_fusion.9
  749.3 8.5 fusion.89
  761.6 12.5 fusion.80
  779.9 187.5 %all_to_all.65 = f32[32,4,128,128]{3,2,1,0:T(8,128)} all-to-all(f32[32,4,128,128]{3,2,1,0:T(8,128)S(1)} %fusion.184), channel_id=1, replica_groups=mesh['gx'=8,'gy'=4] {'gx','gy'}, dimensions={0} | all-to-all | bytes 16777216 | tf_op jit(solution)/shard_map/all_to_all | solution.py:17
  967.4 9.0 copy.226
  976.4 15.8 %fusion.83 = f32[2,2,128,64,64]{2,3,4,1,0:T(8,128)S(1)} fusion(f32[2,2,128,64,64]{2,4,3,1,0:T(8,128)} %bitcast.721, f32[1,64,2,64]{1,3,2,0:T(8,128)S(1)} %get-tuple-element.60, f32[1,64,2,64]{1,3,2,0:T(8,128)S(1)} %get-tuple-element.59), kind=kOutput, calls=%fused_computation.118 | convolution fusion | flops 3221241856 | bytes 16842752 | tf_op jit(solution)/shard_map/c...ab,cadk->d...kb/dot_general | solution.py:33
  995.9 12.5 fusion.86
  1028.8 16.5 %copy.236 = f32[2,128,4096]{1,0,2:T(2,128)} copy(f32[2,128,4096]{1,2,0:T(8,128)S(1)} %bitcast.729) | data formatting | bytes 8388608 | tf_op jit(solution)/shard_map/reshape;reshape | solution.py:82
  1055.6 87.3 %all-to-all-done.4 = f32[2,128,4096]{1,0,2:T(2,128)} async-done(((f32[2,128,4096]{1,0,2:T(2,128)}), f32[2,128,4096]{1,0,2:T(2,128)}, u32[]{:S(2)}, u32[]{:S(2)}) %all-to-all-start.4) | async-done | bytes 4194336 | tf_op jit(solution)/shard_map/all_to_all | solution.py:76
  1198.6 75.9 %all-gather.2.cloned.1.call-done = f32[2,4096,256]{1,2,0:T(8,128)} async-done(((f32[2,128,256]{1,2,0:T(8,128)}), f32[2,4096,256]{1,2,0:T(8,128)}) %all-gather.2.cloned.1.call-update) | async-done | bytes 8388624 | tf_op jit(solution)/shard_map/all_gather | solution.py:171
  (185 shorter events, 230.0 us)
Async XLA Ops:
  14.1 1.6 copy-start.5
  62.6 193.7 %all-to-all-start = ((f32[4,128,4096]{1,0,2:T(4,128)}), f32[4,128,4096]{1,0,2:T(4,128)}, u32[]{:S(2)}, u32[]{:S(2)}) async-start(f32[4,128,4096]{1,0,2:T(4,128)} %copy.179), calls=%async_computation | async-start | bytes 16777216 | tf_op jit(solution)/shard_map/all_to_all | solution.py:76
  309.1 4.5 copy-start
  313.6 5.1 copy-start.2
  612.7 4.0 copy-start.10
  612.7 97.7 %all-to-all-start.2 = ((f32[2,128,4096]{1,0,2:T(2,128)}), f32[2,128,4096]{1,0,2:T(2,128)}, u32[]{:S(2)}, u32[]{:S(2)}) async-start(f32[2,128,4096]{1,0,2:T(2,128)} %copy.207), calls=%async_computation.2 | async-start | bytes 8388608 | tf_op jit(solution)/shard_map/all_to_all | solution.py:76
  730.3 0.9 copy-start.9
  731.2 6.1 copy-start.3
  731.2 6.1 copy-start.6
  731.2 6.1 copy-start.7
  737.3 10.4 copy-start.1
  1045.3 97.6 %all-to-all-start.4 = ((f32[2,128,4096]{1,0,2:T(2,128)}), f32[2,128,4096]{1,0,2:T(2,128)}, u32[]{:S(2)}, u32[]{:S(2)}) async-start(f32[2,128,4096]{1,0,2:T(2,128)} %copy.236), calls=%async_computation.4 | async-start | bytes 8388608 | tf_op jit(solution)/shard_map/all_to_all | solution.py:76
  1049.2 225.3 %all-gather.2.cloned.1.call-start = ((), (), s32[]{:S(2)}) async-start(), calls=%async_computation.5 | async-start | bytes 8650752 | tf_op jit(solution)/shard_map/all_gather | solution.py:171
  1169.4 3.1 slice-start
  1170.0 3.0 slice-start.1
  1170.0 3.6 copy-start.4
  1184.4 1.7 copy-start.8
Sparse Core Ops, SparseCore 0:
  1185.2 89.2 all-gather.1
